TPU v7x, 256 devices: a whole 4x4x8 slice. The times are simulated.
256 devices in a mesh: worker: 16 (over y, z_lo, core), expert: 16 (over z_hi, x).
Axes of the slice: x: 4, y: 4, z: 8 (z_hi: 4, z_lo: 2; z = z_hi * 2 + z_lo), core: 2. Of those that a mesh axis runs over, the one named last changes fastest.
Arguments:
- tokens: bfloat16 [32768, 3072], P(('worker', 'expert')), may hold values from -6 to 6
- route_ids: int32 [32768, 2], P(('worker', 'expert')), may hold values from 0 to 3, as said below
- route_mix: float32 [32768, 2], P(('worker', 'expert')), may hold values from 0.1 to 1
- target: bfloat16 [32768, 3072], P(('worker', 'expert')), may hold values from -6 to 6
- step_count: int32 [16], P('worker'), may hold values from 8 to 101
- gate_weight: bfloat16 [3072, 4096], P(None, 'expert'), may hold values from -0.109375 to 0.109375
- up_weight: bfloat16 [3072, 4096], P(None, 'expert'), may hold values from -0.109375 to 0.109375
- down_weight: bfloat16 [4096, 3072], P('expert'), may hold values from -0.1875 to 0.1875
Outputs:
- outer_gate: float32 [3072, 4096], P('worker', 'expert')
- outer_up: float32 [3072, 4096], P('worker', 'expert')
- outer_down: float32 [4096, 3072], P('expert', 'worker')
- token_loss: float32 [32768], P(('worker', 'expert'))
Inputs may be any that keep to these rules, and one draw needn't show every extreme that they name: `route_ids`: each token's 2 experts differ. In the 128 rows of one device no expert is named by more than 80 rows, and in every device's rows some expert is named by exactly 80.
All inputs are finite; a program needn't handle non-finite values.
Results may differ from a plain program's by a relative error of at most 0.017.
Values may be sent and summed in bfloat16 or wider, within the bound.
A program may use at most 128 MiB of HBM per device.

v0:
```python
import jax
import jax.numpy as jnp
from jax import lax
from jax.sharding import PartitionSpec as P

EXPERTS = 4
CAP = 80


def silu_parts(pre):
    sigmoid_val = jax.nn.sigmoid(pre)
    return (pre * sigmoid_val, sigmoid_val * (1.0 + pre * (1.0 - sigmoid_val)))


def contract_rows(left, right):
    return lax.dot_general(
        left, right, (((0,), (0,)), ((), ())), preferred_element_type=jnp.float32
    )


def expert_forward(inputs, gate_weight, up_weight, down_weight):
    gate_pre = jnp.dot(inputs, gate_weight, preferred_element_type=jnp.float32)
    up_pre = jnp.dot(inputs, up_weight, preferred_element_type=jnp.float32)
    hidden = (gate_pre * jax.nn.sigmoid(gate_pre) * up_pre).astype(jnp.bfloat16)
    partial_out = jnp.dot(hidden, down_weight, preferred_element_type=jnp.float32).astype(
        jnp.bfloat16
    )
    return (gate_pre, up_pre, hidden, partial_out)


def hidden_grads(cotangent, gate_pre, up_pre, down_weight):
    grad_hidden = lax.dot_general(
        cotangent, down_weight, (((1,), (1,)), ((), ())), preferred_element_type=jnp.float32
    )
    activated, slope = silu_parts(gate_pre)
    return (
        (grad_hidden * up_pre * slope).astype(jnp.bfloat16),
        (grad_hidden * activated).astype(jnp.bfloat16),
    )


def per_device(
    tokens, route_ids, route_mix, target, step_count, gate_weight, up_weight, down_weight
):
    tok_dev, width = tokens.shape
    topk = route_ids.shape[1]
    route_total = tok_dev * topk
    expert_devices = lax.axis_size("expert")
    hsplit = expert_devices // EXPERTS
    slot_total = expert_devices * CAP
    flat_ids = route_ids.reshape(-1)
    expert_hit = (flat_ids[:, None] == jnp.arange(EXPERTS, dtype=jnp.int32)[None, :]).astype(
        jnp.int32
    )
    earlier = jnp.cumsum(expert_hit, axis=0) - expert_hit
    slot_index = jnp.sum(earlier * expert_hit, axis=1)
    slot_key = flat_ids * CAP + slot_index
    route_of_slot = (
        jnp.full((EXPERTS * CAP,), route_total, jnp.int32)
        .at[slot_key]
        .set(jnp.arange(route_total, dtype=jnp.int32))
    )
    send_live = route_of_slot < route_total
    safe_route = jnp.minimum(route_of_slot, route_total - 1)
    token_picked = jnp.take(tokens, safe_route // topk, axis=0)
    dispatch_one = jnp.where(
        send_live[:, None], token_picked, jnp.zeros_like(token_picked)
    ).reshape(EXPERTS, CAP, width)
    send_tokens = jnp.broadcast_to(dispatch_one[:, None], (EXPERTS, hsplit, CAP, width)).reshape(
        expert_devices, CAP, width
    )
    arrived = lax.all_to_all(send_tokens, "expert", split_axis=0, concat_axis=0, tiled=True)
    expert_rows = arrived.reshape(slot_total, width)
    gate_pre, up_pre, hidden, partial_slots = expert_forward(
        expert_rows, gate_weight, up_weight, down_weight
    )
    returned = lax.all_to_all(
        partial_slots.reshape(expert_devices, CAP, width),
        "expert",
        split_axis=0,
        concat_axis=0,
        tiled=True,
    )
    expert_out = jnp.sum(
        returned.reshape(EXPERTS, hsplit, CAP, width).astype(jnp.float32), axis=1
    ).reshape(EXPERTS * CAP, width)
    picked_rows = jnp.take(expert_out, slot_key, axis=0).reshape(tok_dev, topk, width)
    mixed_out = jnp.sum(route_mix[:, :, None] * picked_rows, axis=1)
    residual = mixed_out - target.astype(jnp.float32)
    token_loss = 0.5 * jnp.mean(residual * residual, axis=1)
    cot_routes = (
        (route_mix[:, :, None] * residual[:, None, :])
        .astype(jnp.bfloat16)
        .reshape(route_total, width)
    )
    cot_picked = jnp.take(cot_routes, safe_route, axis=0)
    cot_one = jnp.where(send_live[:, None], cot_picked, jnp.zeros_like(cot_picked)).reshape(
        EXPERTS, CAP, width
    )
    send_cot = jnp.broadcast_to(cot_one[:, None], (EXPERTS, hsplit, CAP, width)).reshape(
        expert_devices, CAP, width
    )
    cot_arrived = lax.all_to_all(send_cot, "expert", split_axis=0, concat_axis=0, tiled=True)
    cot_slots = cot_arrived.reshape(slot_total, width)
    weight = step_count[0].astype(jnp.float32)
    total_steps = lax.psum(weight, "worker")
    grad_gate, grad_up = hidden_grads(cot_slots, gate_pre, up_pre, down_weight)
    down_grad, grad_gate, grad_up = (contract_rows(hidden, cot_slots), grad_gate, grad_up)
    gate_grad = contract_rows(expert_rows, grad_gate)
    up_grad = contract_rows(expert_rows, grad_up)
    outer_gate, outer_up, outer_down = (
        lax.psum_scatter(
            (weight * gate_grad).astype(jnp.bfloat16), "worker", scatter_dimension=0, tiled=True
        ).astype(jnp.float32),
        lax.psum_scatter(
            (weight * up_grad).astype(jnp.bfloat16), "worker", scatter_dimension=0, tiled=True
        ).astype(jnp.float32),
        lax.psum_scatter(
            (weight * down_grad).astype(jnp.bfloat16), "worker", scatter_dimension=1, tiled=True
        ).astype(jnp.float32),
    )
    return (outer_gate / total_steps, outer_up / total_steps, outer_down / total_steps, token_loss)


def solution(mesh):
    return jax.shard_map(
        per_device,
        mesh=mesh,
        in_specs=(
            P(("worker", "expert"), None),
            P(("worker", "expert"), None),
            P(("worker", "expert"), None),
            P(("worker", "expert"), None),
            P("worker"),
            P(None, "expert"),
            P(None, "expert"),
            P("expert", None),
        ),
        out_specs=(
            P("worker", "expert"),
            P("worker", "expert"),
            P("expert", "worker"),
            P(("worker", "expert")),
        ),
        check_vma=False,
    )
```

profile of v0, /device:TPU:4, one launch (start us, length us, event | category | flops | bytes accessed | tf_op | source)
XLA Modules:
  0.0 849.6 jit_solution(9377517444615883189)
XLA Ops:
  9.1 1.2 reduce-window.6
  11.0 1.4 scatter_custom_fusion
  14.1 7.3 gather_fusion
  23.4 186.5 %all_to_all.15 = bf16[16,80,3072]{2,1,0:T(8,128)(2,1)S(1)} all-to-all(bf16[16,80,3072]{2,1,0:T(8,128)(2,1)S(1)} %bitcast.48), channel_id=1, replica_groups=mesh['worker'=16,'expert'=16] {'expert'}, dimensions={0} | all-to-all | bytes 15728640 | tf_op jit(solution)/shard_map/all_to_all | solution.py:72
  209.9 2.3 fusion.15
  213.1 3.5 multiply_convert_fusion.3
  216.6 5.3 convolution_convert_fusion
  221.9 7.0 all-to-all-start.1
  229.7 173.6 %all-to-all-done.1 = bf16[16,80,3072]{2,1,0:T(8,128)(2,1)} async-done(((bf16[16,80,3072]{2,1,0:T(8,128)(2,1)}), bf16[16,80,3072]{2,1,0:T(8,128)(2,1)}, u32[]{:S(2)}, u32[]{:S(2)}) %all-to-all-start.1) | async-done | bytes 7864352 | tf_op jit(solution)/shard_map/all_to_all | solution.py:77
  403.3 7.1 convert_reduce_fusion
  410.4 6.9 gather_fusion.1
  417.3 5.2 gather.21
  422.5 7.7 multiply_reduce_fusion
  430.6 2.8 mul.106
  433.4 5.2 mul.107
  438.7 2.2 multiply_convert_fusion
  440.9 3.4 gather_fusion.2
  444.3 1.9 select_select_fusion
  446.2 4.1 broadcast_in_dim.78
  450.3 5.0 all-to-all-start.2
  456.1 168.2 %all-to-all-done.2 = bf16[16,80,3072]{2,1,0:T(8,128)(2,1)} async-done(((bf16[16,80,3072]{2,1,0:T(8,128)(2,1)}), bf16[16,80,3072]{2,1,0:T(8,128)(2,1)}, u32[]{:S(2)}, u32[]{:S(2)}) %all-to-all-start.2) | async-done | bytes 7864352 | tf_op jit(solution)/shard_map/all_to_all | solution.py:103
  624.3 7.6 fusion.2
  632.0 5.6 fusion.16
  638.6 6.9 fusion.1
  645.6 7.7 fusion
  653.3 40.4 %psum.7 = f32[]{:T(128)} all-reduce(f32[]{:T(128)} %bitcast), channel_id=1, replica_groups=mesh['worker'=16,'expert'=16] {'worker'}, use_global_device_ids=true, to_apply=%region_7.8 | all-reduce | flops 1 | bytes 8 | tf_op jit(solution)/shard_map/psum | solution.py:106
  694.3 12.8 %reduce-scatter.8.cloned.1.call-done = bf16[256,192]{0,1:T(8,128)(2,1)} async-done(((bf16[256,3072]{0,1:T(8,128)(2,1)}), bf16[256,192]{0,1:T(8,128)(2,1)}) %reduce-scatter.8.cloned.1.call-update) | async-done | bytes 98320 | tf_op jit(solution)/shard_map/reduce_scatter | solution.py:118
  707.1 2.1 convert_divide_fusion
  709.2 64.6 %reduce-scatter.6.cloned.1.call-done = bf16[192,256]{1,0:T(8,128)(2,1)} async-done(((bf16[3072,256]{1,0:T(8,128)(2,1)}), bf16[192,256]{1,0:T(8,128)(2,1)}) %reduce-scatter.6.cloned.1.call-update) | async-done | bytes 98320 | tf_op jit(solution)/shard_map/reduce_scatter | solution.py:115
  773.9 2.1 convert_divide_fusion.1
  776.0 64.6 %reduce-scatter.4.cloned.1.call-done = bf16[192,256]{1,0:T(8,128)(2,1)} async-done(((bf16[3072,256]{1,0:T(8,128)(2,1)}), bf16[192,256]{1,0:T(8,128)(2,1)}) %reduce-scatter.4.cloned.1.call-update) | async-done | bytes 98320 | tf_op jit(solution)/shard_map/reduce_scatter | solution.py:112
  840.7 2.1 convert_divide_fusion.2
  (68 shorter events, 10.2 us)
Async XLA Ops:
  7.2 209.4 %copy-start = (bf16[256,3072]{1,0:T(8,128)(2,1)S(1)}, bf16[256,3072]{1,0:T(8,128)(2,1)}, u32[]{:S(2)}) copy-start(bf16[256,3072]{1,0:T(8,128)(2,1)} %param.15) | copy-start | bytes 4718596
  23.4 186.5 %copy-start.9 = (bf16[3072,256]{1,0:T(8,128)(2,1)S(1)}, bf16[3072,256]{1,0:T(8,128)(2,1)}, u32[]{:S(2)}) copy-start(bf16[3072,256]{1,0:T(8,128)(2,1)} %param.13) | copy-start | bytes 4718596
  209.9 3.2 copy-start.1
  209.9 3.2 copy-start.10
  213.1 3.5 copy-start.11
  216.6 5.3 copy-start.2
  221.9 7.2 copy-start.5
  221.9 7.4 copy-start.7
  221.9 7.6 copy-start.8
  221.9 181.4 %all-to-all-start.1 = ((bf16[16,80,3072]{2,1,0:T(8,128)(2,1)}), bf16[16,80,3072]{2,1,0:T(8,128)(2,1)}, u32[]{:S(2)}, u32[]{:S(2)}) async-start(bf16[16,80,3072]{2,1,0:T(8,128)(2,1)} %bitcast.46), calls=%async_computation.1 | async-start | bytes 15728640 | tf_op jit(solution)/shard_map/all_to_all | solution.py:77
  422.5 7.8 copy-start.4
  440.9 3.4 copy-start.6
  450.3 174.1 %copy-start.3 = (bf16[1280,256]{1,0:T(8,128)(2,1)S(1)}, bf16[1280,256]{1,0:T(8,128)(2,1)}, u32[]{:S(2)}) copy-start(bf16[1280,256]{1,0:T(8,128)(2,1)} %copy-done.2) | copy-start | bytes 1966084
  450.3 174.1 %all-to-all-start.2 = ((bf16[16,80,3072]{2,1,0:T(8,128)(2,1)}), bf16[16,80,3072]{2,1,0:T(8,128)(2,1)}, u32[]{:S(2)}, u32[]{:S(2)}) async-start(bf16[16,80,3072]{2,1,0:T(8,128)(2,1)} %bitcast.47), calls=%async_computation.2 | async-start | bytes 15728640 | tf_op jit(solution)/shard_map/all_to_all | solution.py:103
  455.2 251.9 %reduce-scatter.8.cloned.1.call-start = ((), (), s32[]{:S(2)}) async-start(), calls=%async_computation.8 | async-start | bytes 1671168 | tf_op jit(solution)/shard_map/reduce_scatter | solution.py:118
  631.9 6.7 copy-start.12
  631.9 141.9 %reduce-scatter.6.cloned.1.call-start = ((), (), s32[]{:S(2)}) async-start(), calls=%async_computation.7 | async-start | bytes 1671168 | tf_op jit(solution)/shard_map/reduce_scatter | solution.py:115
  637.6 1.1 copy-start.13
  645.5 195.1 %reduce-scatter.4.cloned.1.call-start = ((), (), s32[]{:S(2)}) async-start(), calls=%async_computation.6 | async-start | bytes 1671168 | tf_op jit(solution)/shard_map/reduce_scatter | solution.py:112
Sparse Core Ops, SparseCore 0:
  632.1 74.9 reduce-scatter.7
  709.6 64.2 reduce-scatter.5
  776.4 64.2 reduce-scatter.3
where the time goes:
time: 855 us; the launch traced here: 850 us
  waiting for transfers between devices  484 us (57%)
  blocking collectives  227 us (27%)
  local copies, waits for them, and re-layouts  42.9 us (5%)
  matrix products  38.8 us (5%)
  other arithmetic  29.8 us (3%)
  between operations  14.9 us (2%)
  starting transfers between devices  12.3 us (1%)
    all_to_all x1, blocking collectives, per_device(): lax.all_to_all(send_tokens, 'expert', split_axis=0, concat_axis=0, tiled=...  187 us
    all_to_all x1, waiting for transfers between devices, per_device(): lax.all_to_all(partial_slots.reshape(expert_devices, CAP, width), 'expert...  174 us
    all_to_all x1, waiting for transfers between devices, per_device(): lax.all_to_all(send_cot, 'expert', split_axis=0, concat_axis=0, tiled=True)  168 us
    reduce_scatter x1, waiting for transfers between devices, per_device(): lax.psum_scatter((weight * gate_grad).astype(jnp.bfloat16), 'worker', sca...  64.6 us
    reduce_scatter x1, waiting for transfers between devices, per_device(): lax.psum_scatter((weight * up_grad).astype(jnp.bfloat16), 'worker', scatt...  64.6 us
    psum x1, blocking collectives, per_device(): total_steps = lax.psum(weight, 'worker')  40.4 us
    dot_general x3, matrix products, contract_rows(): lax.dot_general(left, right, (((0,), (0,)), ((), ())), preferred_element_...  22.2 us
  transfers between devices with their start and end apart: 5, of which 5 were waited for; matrix products, arithmetic and copies ran while one was open for 3% of the time, Pallas kernels for 0%

commit v1 on v0

--- a/solution.py
+++ b/solution.py
@@ -103,7 +103,7 @@
     cot_arrived = lax.all_to_all(send_cot, "expert", split_axis=0, concat_axis=0, tiled=True)
     cot_slots = cot_arrived.reshape(slot_total, width)
     weight = step_count[0].astype(jnp.float32)
-    total_steps = lax.psum(weight, "worker")
+    total_steps = jnp.sum(lax.all_gather(weight, "worker"), axis=0)
     grad_gate, grad_up = hidden_grads(cot_slots, gate_pre, up_pre, down_weight)
     down_grad, grad_gate, grad_up = (contract_rows(hidden, cot_slots), grad_gate, grad_up)
     gate_grad = contract_rows(expert_rows, grad_gate)

time: 855 us -> 855 us (level)
    psum x1 -> x0, blocking collectives: 40.4 us -> none  [per_device(): total_steps = lax.psum(weight, 'worker')]
    unnamed x0 -> x1, blocking collectives: none -> 39.3 us
where the time goes in v1:
time: 855 us; the launch traced here: 850 us
  waiting for transfers between devices  483 us (56%)
  blocking collectives  226 us (26%)
  local copies, waits for them, and re-layouts  43.5 us (5%)
  matrix products  38.9 us (5%)
  other arithmetic  31.1 us (4%)
  between operations  14.9 us (2%)
  starting transfers between devices  12.3 us (1%)
    all_to_all x1, blocking collectives, per_device(): lax.all_to_all(send_tokens, 'expert', split_axis=0, concat_axis=0, tiled=...  187 us
    all_to_all x1, waiting for transfers between devices, per_device(): lax.all_to_all(partial_slots.reshape(expert_devices, CAP, width), 'expert...  174 us
    all_to_all x1, waiting for transfers between devices, per_device(): lax.all_to_all(send_cot, 'expert', split_axis=0, concat_axis=0, tiled=True)  168 us
    reduce_scatter x1, waiting for transfers between devices, per_device(): lax.psum_scatter((weight * up_grad).astype(jnp.bfloat16), 'worker', scatt...  64.8 us
    reduce_scatter x1, waiting for transfers between devices, per_device(): lax.psum_scatter((weight * gate_grad).astype(jnp.bfloat16), 'worker', sca...  64.6 us
    unnamed x1, blocking collectives  39.3 us
    dot_general x3, matrix products, contract_rows(): lax.dot_general(left, right, (((0,), (0,)), ((), ())), preferred_element_...  22.2 us
  transfers between devices with their start and end apart: 5, of which 5 were waited for; matrix products, arithmetic and copies ran while one was open for 3% of the time, Pallas kernels for 0%

profile of v1, /device:TPU:4, one launch (start us, length us, event | category | flops | bytes accessed | tf_op | source)
XLA Modules:
  0.0 849.8 jit_solution(5556390066564996712)
XLA Ops:
  9.1 1.2 reduce-window.6
  11.0 1.4 scatter_custom_fusion
  14.1 7.3 gather_fusion
  23.4 186.5 %all_to_all.15 = bf16[16,80,3072]{2,1,0:T(8,128)(2,1)S(1)} all-to-all(bf16[16,80,3072]{2,1,0:T(8,128)(2,1)S(1)} %bitcast.49), channel_id=1, replica_groups=mesh['worker'=16,'expert'=16] {'expert'}, dimensions={0} | all-to-all | bytes 15728640 | tf_op jit(solution)/shard_map/all_to_all | solution.py:72
  209.9 2.3 fusion.15
  213.1 3.5 multiply_convert_fusion.3
  216.6 5.3 convolution_convert_fusion
  221.9 7.0 all-to-all-start.1
  229.7 173.6 %all-to-all-done.1 = bf16[16,80,3072]{2,1,0:T(8,128)(2,1)} async-done(((bf16[16,80,3072]{2,1,0:T(8,128)(2,1)}), bf16[16,80,3072]{2,1,0:T(8,128)(2,1)}, u32[]{:S(2)}, u32[]{:S(2)}) %all-to-all-start.1) | async-done | bytes 7864352 | tf_op jit(solution)/shard_map/all_to_all | solution.py:77
  403.3 7.1 convert_reduce_fusion
  410.4 6.9 gather_fusion.1
  417.3 5.2 gather.21
  422.5 7.7 multiply_reduce_fusion
  430.6 2.8 mul.106
  433.4 5.2 mul.107
  438.7 2.2 multiply_convert_fusion
  440.9 3.4 gather_fusion.2
  444.3 1.9 select_select_fusion
  446.2 4.1 broadcast_in_dim.78
  450.3 5.0 all-to-all-start.2
  456.1 168.2 %all-to-all-done.2 = bf16[16,80,3072]{2,1,0:T(8,128)(2,1)} async-done(((bf16[16,80,3072]{2,1,0:T(8,128)(2,1)}), bf16[16,80,3072]{2,1,0:T(8,128)(2,1)}, u32[]{:S(2)}, u32[]{:S(2)}) %all-to-all-start.2) | async-done | bytes 7864352 | tf_op jit(solution)/shard_map/all_to_all | solution.py:103
  624.3 7.6 fusion.2
  632.0 5.6 fusion.16
  638.6 6.9 fusion.1
  645.6 7.7 fusion
  654.7 39.3 %all-reduce = f32[16]{0:T(128)S(1)} all-reduce(f32[16]{0:T(128)S(1)} %convert_dynamic-update-slice_fusion), channel_id=1, replica_groups=mesh['worker'=16,'expert'=16] {'worker'}, use_global_device_ids=true, to_apply=%add | all-reduce | flops 16 | bytes 128
  695.2 11.9 %reduce-scatter.8.cloned.1.call-done = bf16[256,192]{0,1:T(8,128)(2,1)} async-done(((bf16[256,3072]{0,1:T(8,128)(2,1)}), bf16[256,192]{0,1:T(8,128)(2,1)}) %reduce-scatter.8.cloned.1.call-update) | async-done | bytes 98320 | tf_op jit(solution)/shard_map/reduce_scatter | solution.py:118
  707.1 2.1 convert_divide_fusion
  709.3 64.8 %reduce-scatter.6.cloned.1.call-done = bf16[192,256]{1,0:T(8,128)(2,1)} async-done(((bf16[3072,256]{1,0:T(8,128)(2,1)}), bf16[192,256]{1,0:T(8,128)(2,1)}) %reduce-scatter.6.cloned.1.call-update) | async-done | bytes 98320 | tf_op jit(solution)/shard_map/reduce_scatter | solution.py:115
  774.1 2.1 convert_divide_fusion.1
  776.2 64.6 %reduce-scatter.4.cloned.1.call-done = bf16[192,256]{1,0:T(8,128)(2,1)} async-done(((bf16[3072,256]{1,0:T(8,128)(2,1)}), bf16[192,256]{1,0:T(8,128)(2,1)}) %reduce-scatter.4.cloned.1.call-update) | async-done | bytes 98320 | tf_op jit(solution)/shard_map/reduce_scatter | solution.py:112
  840.9 2.1 convert_divide_fusion.2
  (74 shorter events, 12.1 us)
Async XLA Ops:
  7.2 209.4 %copy-start = (bf16[256,3072]{1,0:T(8,128)(2,1)S(1)}, bf16[256,3072]{1,0:T(8,128)(2,1)}, u32[]{:S(2)}) copy-start(bf16[256,3072]{1,0:T(8,128)(2,1)} %param.15) | copy-start | bytes 4718596
  23.4 186.5 %copy-start.9 = (bf16[3072,256]{1,0:T(8,128)(2,1)S(1)}, bf16[3072,256]{1,0:T(8,128)(2,1)}, u32[]{:S(2)}) copy-start(bf16[3072,256]{1,0:T(8,128)(2,1)} %param.13) | copy-start | bytes 4718596
  209.9 3.2 copy-start.1
  209.9 3.2 copy-start.10
  213.1 3.5 copy-start.12
  216.6 5.3 copy-start.2
  221.9 7.2 copy-start.5
  221.9 7.4 copy-start.7
  221.9 7.6 copy-start.8
  221.9 181.4 %all-to-all-start.1 = ((bf16[16,80,3072]{2,1,0:T(8,128)(2,1)}), bf16[16,80,3072]{2,1,0:T(8,128)(2,1)}, u32[]{:S(2)}, u32[]{:S(2)}) async-start(bf16[16,80,3072]{2,1,0:T(8,128)(2,1)} %bitcast.47), calls=%async_computation.1 | async-start | bytes 15728640 | tf_op jit(solution)/shard_map/all_to_all | solution.py:77
  422.5 7.8 copy-start.4
  440.9 3.4 copy-start.6
  450.3 174.1 %copy-start.3 = (bf16[1280,256]{1,0:T(8,128)(2,1)S(1)}, bf16[1280,256]{1,0:T(8,128)(2,1)}, u32[]{:S(2)}) copy-start(bf16[1280,256]{1,0:T(8,128)(2,1)} %copy-done.2) | copy-start | bytes 1966084
  450.3 174.1 %all-to-all-start.2 = ((bf16[16,80,3072]{2,1,0:T(8,128)(2,1)}), bf16[16,80,3072]{2,1,0:T(8,128)(2,1)}, u32[]{:S(2)}, u32[]{:S(2)}) async-start(bf16[16,80,3072]{2,1,0:T(8,128)(2,1)} %bitcast.48), calls=%async_computation.2 | async-start | bytes 15728640 | tf_op jit(solution)/shard_map/all_to_all | solution.py:103
  455.2 251.9 %reduce-scatter.8.cloned.1.call-start = ((), (), s32[]{:S(2)}) async-start(), calls=%async_computation.8 | async-start | bytes 1671168 | tf_op jit(solution)/shard_map/reduce_scatter | solution.py:118
  631.9 6.7 copy-start.13
  631.9 142.2 %reduce-scatter.6.cloned.1.call-start = ((), (), s32[]{:S(2)}) async-start(), calls=%async_computation.7 | async-start | bytes 1671168 | tf_op jit(solution)/shard_map/reduce_scatter | solution.py:115
  637.6 1.1 copy-start.14
  645.6 195.3 %reduce-scatter.4.cloned.1.call-start = ((), (), s32[]{:S(2)}) async-start(), calls=%async_computation.6 | async-start | bytes 1671168 | tf_op jit(solution)/shard_map/reduce_scatter | solution.py:112
  645.6 7.8 copy-start.11
Sparse Core Ops, SparseCore 0:
  632.1 75.0 reduce-scatter.7
  709.6 64.4 reduce-scatter.5
  776.6 64.2 reduce-scatter.3
